TPU v7x, 256 devices: a whole 4x4x8 slice. The times are simulated.
256 devices in a mesh: scene: 8 (over x, core), region: 32 (over z, y).
Axes of the slice: x: 4, y: 4, z: 8, core: 2. Of those that a mesh axis runs over, the one named last changes fastest.
Arguments:
- tiles: bfloat16 [8, 64, 32, 32, 256], P('scene', 'region'), may hold values from -6 to 6
- cotangent: bfloat16 [8, 64, 16, 16, 256], P('scene', 'region'), may hold values from -6 to 6
- positions: int32 [8, 64], P('scene', 'region'), may hold values from 0 to 63, each once within a row
- clear: int32 [8, 64], P('scene', 'region'), may hold values 0 or 1
- w_first: bfloat16 [2304, 256], P('scene'), may hold values from -0.125 to 0.125
- w_second: bfloat16 [2304, 256], P('scene'), may hold values from -0.125 to 0.125
Outputs:
- features: bfloat16 [8, 64, 16, 16, 256], P('scene', 'region')
- grad_first: float32 [2304, 256], P('region', 'scene')
- grad_second: float32 [2304, 256], P('region', 'scene')
Inputs may be any that keep to these rules, and one draw needn't show every extreme that they name: Each scene's row is a permutation of the grid positions 0 to 63.
All inputs are finite; a program needn't handle non-finite values. No bound on the sum of `clear` on one device may be relied on, other than what follows from the above.
Results may differ from a plain program's by a relative error of at most 0.005.
Values may be sent and summed in bfloat16 or wider, within the bound.
A program may use at most 128 MiB of HBM per device.

v0:
```python
import math
import jax
import jax.numpy as jnp
from jax import lax
from jax.sharding import PartitionSpec as P

GW = 4


def silu_slope(pre_act):
    sigmoid_v = jax.nn.sigmoid(pre_act)
    return sigmoid_v * (1.0 + pre_act * (1.0 - sigmoid_v))


def tap_patches(padded, out_side, stride):
    windows = []
    for tap_row in range(3):
        for tap_col in range(3):
            windows.append(
                padded[
                    :,
                    tap_row : tap_row + stride * out_side : stride,
                    tap_col : tap_col + stride * out_side : stride,
                    :,
                ]
            )
    stacked = jnp.concatenate(windows, axis=-1)
    return stacked.reshape(-1, stacked.shape[-1])


def shift_down(values, axis_num):
    widths = [(0, 0)] * values.ndim
    widths[axis_num] = (1, 0)
    padded = jnp.pad(values, widths)
    return lax.slice_in_dim(padded, 0, values.shape[axis_num], 1, axis_num)


def local(tiles, cotangent, positions, clear, w_first, w_second):
    tiles_here = tiles[0]
    slot_count = tiles_here.shape[0]
    tile_side = tiles_here.shape[1]
    tile_half = tile_side // 2
    channels = tiles_here.shape[3]
    local_pos = positions[0]
    every_pos = lax.all_gather(positions, "region", axis=1, tiled=True)[0]
    tile_count = every_pos.shape[0]
    grid_rows = tile_count // GW
    slot_ids = jnp.arange(tile_count, dtype=jnp.int32)
    onehot = (every_pos[:, None] == slot_ids[None, :]).astype(jnp.int32)
    slot_of = jnp.sum(onehot * slot_ids[:, None], axis=0)
    row_here = local_pos // GW
    col_here = local_pos % GW

    def fetch(all_rims, down, sideways, which):
        new_row = row_here + down
        new_col = col_here + sideways
        inside = (new_row >= 0) & (new_row < grid_rows) & (new_col >= 0) & (new_col < GW)
        position = jnp.clip(new_row, 0, grid_rows - 1) * GW + jnp.clip(new_col, 0, GW - 1)
        picked = jnp.take(all_rims, jnp.take(slot_of, position), axis=0)[:, which]
        return picked * inside.astype(picked.dtype)[:, None, None]

    edge_rims = jnp.stack(
        [
            tiles_here[:, 0],
            tiles_here[:, tile_side - 1],
            tiles_here[:, :, 0],
            tiles_here[:, :, tile_side - 1],
        ],
        axis=1,
    )
    all_edges = lax.all_gather(edge_rims, "region", axis=0, tiled=True)
    above_row = fetch(all_edges, -1, 0, 1)
    below_row = fetch(all_edges, 1, 0, 0)
    left_col = fetch(all_edges, 0, -1, 3)
    right_col = fetch(all_edges, 0, 1, 2)
    corner_ul = fetch(all_edges, -1, -1, 1)[:, tile_side - 1]
    corner_ur = fetch(all_edges, -1, 1, 1)[:, 0]
    corner_dl = fetch(all_edges, 1, -1, 0)[:, tile_side - 1]
    corner_dr = fetch(all_edges, 1, 1, 0)[:, 0]
    upper = jnp.concatenate([corner_ul[:, None], above_row, corner_ur[:, None]], axis=1)
    lower = jnp.concatenate([corner_dl[:, None], below_row, corner_dr[:, None]], axis=1)
    middle = jnp.concatenate([left_col[:, :, None], tiles_here, right_col[:, :, None]], axis=2)
    input_pad = jnp.concatenate([upper[:, None], middle, lower[:, None]], axis=1)
    patches_first = tap_patches(input_pad, tile_side, 1)
    pre_flat = jnp.dot(
        patches_first,
        lax.all_gather(w_first, "scene", axis=0, tiled=True),
        preferred_element_type=jnp.float32,
    )
    second_full = lax.all_gather(w_second, "scene", axis=0, tiled=True)
    pre_act = pre_flat.reshape(slot_count, tile_side, tile_side, channels)
    hidden = jax.nn.silu(pre_act).astype(jnp.bfloat16)
    hidden_rims = jnp.stack([hidden[:, tile_side - 1], hidden[:, :, tile_side - 1]], axis=1)
    all_hidden = lax.all_gather(hidden_rims, "region", axis=0, tiled=True)
    hidden_above = fetch(all_hidden, -1, 0, 0)
    hidden_left = fetch(all_hidden, 0, -1, 1)
    hidden_corner = fetch(all_hidden, -1, -1, 0)[:, tile_side - 1]
    hidden_top = jnp.concatenate([hidden_corner[:, None], hidden_above], axis=1)
    hidden_body = jnp.concatenate([hidden_left[:, :, None], hidden], axis=2)
    hidden_pad = jnp.concatenate([hidden_top[:, None], hidden_body], axis=1)
    patches_second = tap_patches(hidden_pad, tile_half, 2)
    out_flat = jnp.dot(patches_second, second_full, preferred_element_type=jnp.float32)
    features = out_flat.astype(jnp.bfloat16).reshape(1, slot_count, tile_half, tile_half, channels)
    masked = cotangent[0] * clear[0].astype(jnp.bfloat16)[:, None, None, None]
    masked_flat = masked.reshape(-1, channels)
    grad_second = lax.dot_general(
        patches_second, masked_flat, (((0,), (0,)), ((), ())), preferred_element_type=jnp.float32
    )
    grad_rims = jnp.stack([masked[:, 0], masked[:, :, 0]], axis=1)
    all_grads = lax.all_gather(grad_rims, "region", axis=0, tiled=True)
    grad_below = fetch(all_grads, 1, 0, 0)
    grad_right = fetch(all_grads, 0, 1, 1)
    grad_corner = fetch(all_grads, 1, 1, 0)[:, 0]
    grad_body = jnp.concatenate([masked, grad_right[:, :, None]], axis=2)
    grad_bottom = jnp.concatenate([grad_below, grad_corner[:, None]], axis=1)
    grad_pad = jnp.concatenate([grad_body, grad_bottom[:, None]], axis=1)
    extended = tile_half + 1
    spread = lax.dot_general(
        grad_pad.reshape(-1, channels),
        second_full,
        (((1,), (1,)), ((), ())),
        preferred_element_type=jnp.float32,
    )
    spread = spread.reshape(slot_count, extended, extended, 3, 3, channels)
    row_even = spread[:, :, :, 0] + shift_down(spread[:, :, :, 2], 1)
    row_odd = spread[:, :, :, 1]
    by_rows = jnp.stack([row_even, row_odd], axis=2).reshape(
        slot_count, 2 * extended, extended, 3, channels
    )
    col_even = by_rows[:, :, :, 0] + shift_down(by_rows[:, :, :, 2], 2)
    col_odd = by_rows[:, :, :, 1]
    dense = jnp.stack([col_even, col_odd], axis=3).reshape(
        slot_count, 2 * extended, 2 * extended, channels
    )
    dhidden = dense[:, 1 : tile_side + 1, 1 : tile_side + 1]
    dpre = (dhidden * silu_slope(pre_act)).astype(jnp.bfloat16)
    grad_first = lax.dot_general(
        patches_first,
        dpre.reshape(-1, channels),
        (((0,), (0,)), ((), ())),
        preferred_element_type=jnp.float32,
    )
    row_block = grad_first.shape[0] // lax.axis_size("region")
    full_first, full_second = lax.psum((grad_first, grad_second), "region")
    sum_sq = jnp.sum(full_first * full_first) + jnp.sum(full_second * full_second)
    row_start = lax.axis_index("region") * row_block
    share_first = lax.dynamic_slice_in_dim(full_first, row_start, row_block, 0)
    share_second = lax.dynamic_slice_in_dim(full_second, row_start, row_block, 0)
    factor = 3.0 * channels * math.sqrt(2.0) / (jnp.sqrt(sum_sq) + 0.01) / lax.axis_size("scene")
    out_first, out_second = (
        lax.psum_scatter(factor * share_first, "scene", scatter_dimension=1, tiled=True),
        lax.psum_scatter(factor * share_second, "scene", scatter_dimension=1, tiled=True),
    )
    return (features, out_first, out_second)


def solution(mesh):
    in_specs = (
        P("scene", "region", None, None, None),
        P("scene", "region", None, None, None),
        P("scene", "region"),
        P("scene", "region"),
        P("scene", None),
        P("scene", None),
    )
    out_specs = (P("scene", "region", None, None, None), P("region", "scene"), P("region", "scene"))
    return jax.shard_map(local, mesh=mesh, in_specs=in_specs, out_specs=out_specs, check_vma=False)
```

profile of v0, /device:TPU:8, one launch (start us, length us, event | category | flops | bytes accessed | tf_op | source)
XLA Modules:
  0.0 681.8 jit_solution(13259119407148330793)
XLA Ops:
  10.5 1.1 fusion.37
  13.7 1.2 and_convert_fusion.2
  15.0 1.3 dynamic-slice
  17.6 22.6 %all-reduce.2 = s32[64]{0:T(128)S(1)} all-reduce(s32[64]{0:T(128)S(1)} %bitcast_dynamic-update-slice_fusion), channel_id=1, replica_groups=mesh['scene'=8,'region'=32] {'region'}, use_global_device_ids=true, to_apply=%add.2 | all-reduce | flops 64 | bytes 512
  50.9 37.8 %all-gather.14.cloned.1.call-done = bf16[64,2,16,256]{3,2,1,0:T(8,128)(2,1)} async-done(((bf16[2,2,16,256]{3,2,1,0:T(8,128)(2,1)}), bf16[64,2,16,256]{3,2,1,0:T(8,128)(2,1)}) %all-gather.14.cloned.1.call-update) | async-done | bytes 1048592 | tf_op jit(solution)/shard_map/all_gather | solution.py:110
  88.7 1.8 gather_fusion.21
  90.6 1.8 gather_fusion.19
  92.5 1.8 gather_fusion.20
  94.4 76.7 %all-gather.6.cloned.1.call-done = bf16[64,4,32,256]{3,2,1,0:T(8,128)(2,1)} async-done(((bf16[2,4,32,256]{3,2,1,0:T(8,128)(2,1)}), bf16[64,4,32,256]{3,2,1,0:T(8,128)(2,1)}) %all-gather.6.cloned.1.call-update) | async-done | bytes 4194320 | tf_op jit(solution)/shard_map/all_gather | solution.py:71
  171.1 2.7 gather_fusion.15
  174.6 23.1 %all-gather.12.cloned.1.call-done = bf16[2304,256]{1,0:T(8,128)(2,1)} async-done(((bf16[288,256]{1,0:T(8,128)(2,1)}), bf16[2304,256]{1,0:T(8,128)(2,1)}) %all-gather.12.cloned.1.call-update) | async-done | bytes 1179664 | tf_op jit(solution)/shard_map/all_gather | solution.py:90
  197.6 2.5 fusion.11
  200.4 1.8 fusion.1
  202.2 3.6 gather_fusion.13
  205.8 1.4 fusion.21
  207.3 3.5 gather_fusion.9
  211.6 1.3 copy_multiply_fusion.2
  212.9 3.5 gather_fusion.1
  217.3 1.3 slice_multiply_fusion.5
  218.6 3.6 gather_fusion.5
  223.0 1.3 slice_multiply_fusion.4
  224.3 3.5 gather_fusion.11
  228.7 1.2 slice_multiply_fusion.3
  229.9 3.5 gather_fusion.7
  234.3 1.4 copy_multiply_fusion.3
  235.7 3.5 gather_fusion.3
  241.5 2.8 pad_maximum_fusion.2
  244.4 1.2 slice_dynamic-update-slice_fusion.5
  246.0 3.6 copy.128
  249.6 3.7 copy.138
  253.3 1.6 slice_dynamic-update-slice_fusion.4
  254.9 1.6 slice_dynamic-update-slice_fusion.3
  256.5 1.6 fusion.9
  259.2 1.7 fusion.8
  260.9 1.2 slice_dynamic-update-slice_fusion.2
  262.1 1.7 slice_dynamic-update-slice_fusion.1
  263.8 1.6 slice_dynamic-update-slice_fusion
  265.3 8.0 %multiply_convert_fusion = (bf16[2,32,32,256]{3,2,1,0:T(8,128)(2,1)S(1)}, f32[2,32,32,256]{3,2,1,0:T(8,128)}) fusion(bf16[2,32,32,2304]{3,2,1,0:T(8,128)(2,1)} %slice_dynamic-update-slice_fusion, bf16[2304,256]{1,0:T(8,128)(2,1)} %all-gather.8.cloned.1.call-done), kind=kOutput, calls=%fused_computation.36 | convolution fusion | flops 2418540544 | bytes 13762560 | tf_op jit(solution)/shard_map/dot_general | solution.py:85
  273.5 9.9 %slice.204 = bf16[2,16,16,256]{3,2,1,0:T(8,128)(2,1)} slice(bf16[2,32,32,256]{3,2,1,0:T(8,128)(2,1)S(1)} %get-tuple-element.70), slice={[0:2:1], [0:32:2], [0:32:2], [0:256:1]} | slice | bytes 524288 | tf_op jit(solution)/shard_map/slice | solution.py:20
  283.4 9.8 %slice.205 = bf16[2,16,16,256]{3,2,1,0:T(8,128)(2,1)} slice(bf16[2,32,32,256]{3,2,1,0:T(8,128)(2,1)S(1)} %get-tuple-element.70), slice={[0:2:1], [0:32:2], [1:32:2], [0:256:1]} | slice | bytes 524288 | tf_op jit(solution)/shard_map/slice | solution.py:20
  293.2 9.8 %slice.207 = bf16[2,16,16,256]{3,2,1,0:T(8,128)(2,1)} slice(bf16[2,32,32,256]{3,2,1,0:T(8,128)(2,1)S(1)} %get-tuple-element.70), slice={[0:2:1], [1:32:2], [0:32:2], [0:256:1]} | slice | bytes 524288 | tf_op jit(solution)/shard_map/slice | solution.py:20
  303.0 9.8 %slice.208 = bf16[2,16,16,256]{3,2,1,0:T(8,128)(2,1)} slice(bf16[2,32,32,256]{3,2,1,0:T(8,128)(2,1)S(1)} %get-tuple-element.70), slice={[0:2:1], [1:32:2], [1:32:2], [0:256:1]} | slice | bytes 524288 | tf_op jit(solution)/shard_map/slice | solution.py:20
  312.8 2.4 slice_bitcast_fusion.3
  316.0 2.2 fusion.4
  319.3 1.1 slice.308
  320.9 7.9 %convolution_bitcast_fusion.1 = f32[2304,256]{1,0:T(8,128)} fusion(bf16[2,32,32,2304]{3,2,1,0:T(8,128)(2,1)} %slice_dynamic-update-slice_fusion, f32[2,32,32,256]{3,0,2,1:T(2,128)S(1)} %slice.308, f32[2,32,32,256]{3,2,1,0:T(8,128)S(1)} %copy-done.25), kind=kOutput, calls=%fused_computation.24 | convolution fusion | flops 2420637696 | bytes 15990784 | tf_op jit(solution)/shard_map/dot_general | solution.py:137
  328.8 64.2 %all-gather.10.cloned.1.call-done = bf16[64,2,32,256]{3,2,1,0:T(8,128)(2,1)} async-done(((bf16[2,2,32,256]{3,2,1,0:T(8,128)(2,1)}), bf16[64,2,32,256]{3,2,1,0:T(8,128)(2,1)}) %all-gather.10.cloned.1.call-update) | async-done | bytes 2097168 | tf_op jit(solution)/shard_map/all_gather | solution.py:94
  393.0 2.3 gather_fusion.18
  395.5 1.8 pad_maximum_fusion.3
  397.4 2.3 gather_fusion.16
  399.8 2.3 gather_fusion.17
  405.7 12.5 %slice.203 = bf16[2,16,16,256]{3,2,1,0:T(8,128)(2,1)S(1)} slice(bf16[2,32,33,256]{3,2,1,0:T(8,128)(2,1)} %pad_maximum_fusion.3), slice={[0:2:1], [0:32:2], [0:32:2], [0:256:1]} | slice | bytes 524288 | tf_op jit(solution)/shard_map/slice | solution.py:20
  418.3 12.5 %slice.206 = bf16[2,16,16,256]{3,2,1,0:T(8,128)(2,1)S(1)} slice(bf16[2,32,33,256]{3,2,1,0:T(8,128)(2,1)} %pad_maximum_fusion.3), slice={[0:2:1], [1:32:2], [0:32:2], [0:256:1]} | slice | bytes 524288 | tf_op jit(solution)/shard_map/slice | solution.py:20
  431.1 1.4 copy-done.12
  432.5 2.3 convolution_bitcast_fusion
  434.9 164.7 %all-reduce.6.cloned.1.call-done = (f32[2304,256]{1,0:T(8,128)}, f32[2304,256]{1,0:T(8,128)}) async-done(((f32[2304,256]{1,0:T(8,128)}, f32[2304,256]{1,0:T(8,128)}), (f32[2304,256]{1,0:T(8,128)}, f32[2304,256]{1,0:T(8,128)})) %all-reduce.6.cloned.1.call-update) | async-done | bytes 4718608 | tf_op jit(solution)/shard_map/psum | solution.py:144
  599.6 3.0 multiply_reduce_fusion
  602.7 1.2 multiply_reduce_fusion.1
  605.2 1.5 dynamic-slice_multiply_fusion
  606.8 1.6 copy.141
  609.1 1.6 copy.139
  610.8 3.1 convolution_convert_fusion
  613.9 26.2 %reduce-scatter.9.cloned.1.call-done = f32[32,72]{1,0:T(8,128)} async-done(((f32[256,72]{1,0:T(8,128)}), f32[32,72]{1,0:T(8,128)}) %reduce-scatter.9.cloned.1.call-update) | async-done | bytes 9232
  640.2 34.8 %reduce-scatter.7.cloned.1.call-done = f32[32,72]{1,0:T(8,128)} async-done(((f32[256,72]{1,0:T(8,128)}), f32[32,72]{1,0:T(8,128)}) %reduce-scatter.7.cloned.1.call-update) | async-done | bytes 9232
  (153 shorter events, 33.2 us)
Async XLA Ops:
  7.2 81.6 %all-gather.14.cloned.1.call-start = ((), (), s32[]{:S(2)}) async-start(), calls=%async_computation.6 | async-start | bytes 1081344 | tf_op jit(solution)/shard_map/all_gather | solution.py:110
  8.9 188.7 %copy-start.3 = (bf16[2,16,16,256]{3,2,1,0:T(8,128)(2,1)}, bf16[2,16,16,256]{3,2,1,0:T(8,128)(2,1)S(1)}, u32[]{:S(2)}) copy-start(bf16[2,16,16,256]{3,2,1,0:T(8,128)(2,1)S(1)} %bitcast_multiply_fusion) | copy-start | bytes 786436
  9.7 161.4 %all-gather.6.cloned.1.call-start = ((), (), s32[]{:S(2)}) async-start(), calls=%async_computation.2 | async-start | bytes 4325376 | tf_op jit(solution)/shard_map/all_gather | solution.py:71
  12.4 185.3 %all-gather.12.cloned.1.call-start = ((), (), s32[]{:S(2)}) async-start(), calls=%async_computation.5 | async-start | bytes 1327104 | tf_op jit(solution)/shard_map/all_gather | solution.py:90
  13.1 252.2 %all-gather.8.cloned.1.call-start = ((), (), s32[]{:S(2)}) async-start(), calls=%async_computation.3 | async-start | bytes 1327104 | tf_op jit(solution)/shard_map/all_gather | solution.py:87
  13.7 379.4 %all-gather.10.cloned.1.call-start = ((), (), s32[]{:S(2)}) async-start(), calls=%async_computation.4 | async-start | bytes 2162688 | tf_op jit(solution)/shard_map/all_gather | solution.py:94
  41.7 52.8 %copy-start.20 = (pred[2]{0:T(512)(128)(4,1)}, pred[2]{0:T(512)(128)(4,1)S(1)}, u32[]{:S(2)}) copy-start(pred[2]{0:T(512)(128)(4,1)S(1)} %get-tuple-element.74) | copy-start | bytes 10
  42.9 51.4 %copy-start.21 = (bf16[2]{0:T(256)(128)(2,1)}, bf16[2]{0:T(256)(128)(2,1)S(1)}, u32[]{:S(2)}) copy-start(bf16[2]{0:T(256)(128)(2,1)S(1)} %get-tuple-element.78) | copy-start | bytes 16
  42.9 51.4 %copy-start.22 = (pred[2]{0:T(512)(128)(4,1)}, pred[2]{0:T(512)(128)(4,1)S(1)}, u32[]{:S(2)}) copy-start(pred[2]{0:T(512)(128)(4,1)S(1)} %get-tuple-element.41) | copy-start | bytes 10
  42.9 51.5 %copy-start.23 = (bf16[2]{0:T(256)(128)(2,1)}, bf16[2]{0:T(256)(128)(2,1)S(1)}, u32[]{:S(2)}) copy-start(bf16[2]{0:T(256)(128)(2,1)S(1)} %get-tuple-element.82) | copy-start | bytes 16
  43.0 51.4 %copy-start.14 = (s32[1024]{0:T(1024)}, s32[1024]{0:T(1024)S(1)}, u32[]{:S(2)}) copy-start(s32[1024]{0:T(1024)S(1)} %pad_clamp_fusion.2) | copy-start | bytes 12292
  43.0 49.4 %copy-start.13 = (s32[1024]{0:T(1024)}, s32[1024]{0:T(1024)S(1)}, u32[]{:S(2)}) copy-start(s32[1024]{0:T(1024)S(1)} %pad_clamp_fusion.6) | copy-start | bytes 12292
  202.2 39.3 %copy-start = (bf16[1,2,32,32,256]{4,3,2,1,0:T(8,128)(2,1)S(1)}, bf16[1,2,32,32,256]{4,3,2,1,0:T(8,128)(2,1)}, u32[]{:S(2)}) copy-start(bf16[1,2,32,32,256]{4,3,2,1,0:T(8,128)(2,1)} %param.14) | copy-start | bytes 3145732
  241.5 4.1 copy-start.1
  253.3 3.3 copy-start.11
  256.5 2.7 copy-start.10
  316.0 283.7 %all-reduce.6.cloned.1.call-start = ((), (), s32[]{:S(2)}) async-start(), calls=%async_computation.9 | async-start | bytes 9437184 | tf_op jit(solution)/shard_map/psum | solution.py:144
  319.3 1.6 copy-start.25
  320.9 74.4 %copy-start.19 = (pred[2]{0:T(512)(128)(4,1)S(1)}, pred[2]{0:T(512)(128)(4,1)}, u32[]{:S(2)}) copy-start(pred[2]{0:T(512)(128)(4,1)} %get-tuple-element.39) | copy-start | bytes 10
  320.9 74.5 %copy-start.17 = (bf16[2]{0:T(256)(128)(2,1)S(1)}, bf16[2]{0:T(256)(128)(2,1)}, u32[]{:S(2)}) copy-start(bf16[2]{0:T(256)(128)(2,1)} %get-tuple-element.81) | copy-start | bytes 16
  328.8 70.8 %copy-start.18 = (pred[2]{0:T(512)(128)(4,1)S(1)}, pred[2]{0:T(512)(128)(4,1)}, u32[]{:S(2)}) copy-start(pred[2]{0:T(512)(128)(4,1)} %get-tuple-element.33) | copy-start | bytes 10
  328.8 70.9 %copy-start.24 = (bf16[2]{0:T(256)(128)(2,1)S(1)}, bf16[2]{0:T(256)(128)(2,1)}, u32[]{:S(2)}) copy-start(bf16[2]{0:T(256)(128)(2,1)} %get-tuple-element.80) | copy-start | bytes 16
  328.8 73.2 %copy-start.15 = (pred[2]{0:T(512)(128)(4,1)S(1)}, pred[2]{0:T(512)(128)(4,1)}, u32[]{:S(2)}) copy-start(pred[2]{0:T(512)(128)(4,1)} %get-tuple-element.35) | copy-start | bytes 10
  328.8 73.3 %copy-start.16 = (bf16[2]{0:T(256)(128)(2,1)S(1)}, bf16[2]{0:T(256)(128)(2,1)}, u32[]{:S(2)}) copy-start(bf16[2]{0:T(256)(128)(2,1)} %get-tuple-element.76) | copy-start | bytes 16
  402.9 28.0 %copy-start.9 = (bf16[2,16,16,256]{3,2,1,0:T(8,128)(2,1)S(1)}, bf16[2,16,16,256]{3,2,1,0:T(8,128)(2,1)}, u32[]{:S(2)}) copy-start(bf16[2,16,16,256]{3,2,1,0:T(8,128)(2,1)} %slice.204) | copy-start | bytes 786436
  403.8 27.2 %copy-start.8 = (bf16[2,16,16,256]{3,2,1,0:T(8,128)(2,1)S(1)}, bf16[2,16,16,256]{3,2,1,0:T(8,128)(2,1)}, u32[]{:S(2)}) copy-start(bf16[2,16,16,256]{3,2,1,0:T(8,128)(2,1)} %slice.205) | copy-start | bytes 786436
  405.7 25.3 %copy-start.7 = (bf16[2,16,16,256]{3,2,1,0:T(8,128)(2,1)S(1)}, bf16[2,16,16,256]{3,2,1,0:T(8,128)(2,1)}, u32[]{:S(2)}) copy-start(bf16[2,16,16,256]{3,2,1,0:T(8,128)(2,1)} %slice.207) | copy-start | bytes 786436
  418.3 12.8 %copy-start.6 = (bf16[2,16,16,256]{3,2,1,0:T(8,128)(2,1)S(1)}, bf16[2,16,16,256]{3,2,1,0:T(8,128)(2,1)}, u32[]{:S(2)}) copy-start(bf16[2,16,16,256]{3,2,1,0:T(8,128)(2,1)} %slice.208) | copy-start | bytes 786436
  430.8 1.7 copy-start.4
  431.1 1.4 copy-start.12
  434.8 205.3 %reduce-scatter.9.cloned.1.call-start = ((), (), s32[]{:S(2)}) async-start(), calls=%async_computation.8 | async-start | bytes 147456
  599.6 3.0 copy-start.2
  599.6 11.2 %copy-start.5 = (bf16[2304,256]{1,0:T(8,128)(2,1)S(1)}, bf16[2304,256]{1,0:T(8,128)(2,1)}, u32[]{:S(2)}) copy-start(bf16[2304,256]{1,0:T(8,128)(2,1)} %all-gather.12.cloned.1.call-done) | copy-start | bytes 3538948
  608.4 66.6 %reduce-scatter.7.cloned.1.call-start = ((), (), s32[]{:S(2)}) async-start(), calls=%async_computation.7 | async-start | bytes 147456
Sparse Core Ops, SparseCore 0:
  10.6 78.0 all-gather.13
  91.9 79.1 all-gather.5
  172.9 24.6 all-gather.11
  199.3 26.2 all-gather.7
  316.1 76.9 all-gather.9
  435.0 164.6 all-reduce.5
  608.5 31.5 reduce-scatter.8
  643.2 31.6 reduce-scatter.6
where the time goes:
time: 686 us; the launch traced here: 682 us
  waiting for transfers between devices  429 us (63%)
  local copies, waits for them, and re-layouts  143 us (21%)
  other arithmetic  46.8 us (7%)
  matrix products  23.9 us (3%)
  blocking collectives  22.6 us (3%)
  between operations  16.8 us (2%)
    psum x1, waiting for transfers between devices, local(): full_first, full_second = lax.psum((grad_first, grad_second), 'region')  165 us
    all_gather x1, waiting for transfers between devices, local(): all_edges = lax.all_gather(edge_rims, 'region', axis=0, tiled=True)  76.7 us
    slice x9, local copies, waits for them, and re-layouts, tap_patches(): padded[:, tap_row:tap_row + stride * out_side:stride, tap_col:tap_col + s...  67.2 us
    all_gather x1, waiting for transfers between devices, local(): all_hidden = lax.all_gather(hidden_rims, 'region', axis=0, tiled=True)  64.2 us
    unnamed x10, waiting for transfers between devices  62.3 us
    gather x22, local copies, waits for them, and re-layouts, fetch(): picked = jnp.take(all_rims, jnp.take(slot_of, position), axis=0)[:, which]  44.7 us
    all_gather x1, waiting for transfers between devices, local(): all_grads = lax.all_gather(grad_rims, 'region', axis=0, tiled=True)  37.8 us
    all_gather x1, waiting for transfers between devices, local(): second_full = lax.all_gather(w_second, 'scene', axis=0, tiled=True)  23.1 us
  transfers between devices with their start and end apart: 8, of which 7 were waited for; matrix products, arithmetic and copies ran while one was open for 16% of the time, Pallas kernels for 0%

commit v1 on v0

--- a/solution.py
+++ b/solution.py
@@ -87,7 +87,14 @@
         lax.all_gather(w_first, "scene", axis=0, tiled=True),
         preferred_element_type=jnp.float32,
     )
-    second_full = lax.all_gather(w_second, "scene", axis=0, tiled=True)
+    ring = [w_second]
+    for hop in range(7):
+        ring.append(lax.ppermute(ring[-1], "scene", [(dev, (dev + 1) % 8) for dev in range(8)]))
+    second_full = jnp.roll(
+        jnp.concatenate(ring[::-1], axis=0),
+        (lax.axis_index("scene") + 1) * ring[0].shape[0],
+        axis=0,
+    )
     pre_act = pre_flat.reshape(slot_count, tile_side, tile_side, channels)
     hidden = jax.nn.silu(pre_act).astype(jnp.bfloat16)
     hidden_rims = jnp.stack([hidden[:, tile_side - 1], hidden[:, :, tile_side - 1]], axis=1)

time: 686 us -> 660 us (0.962)
  waiting for transfers between devices: 429 us -> 403 us
    all_gather x1, waiting for transfers between devices: 37.8 us -> 7.2 us  [local(): all_grads = lax.all_gather(grad_rims, 'region', axis=0, tiled=True)]
    ppermute x0 -> x7, waiting for transfers between devices: none -> 30.5 us  [local(): lax.ppermute(ring[-1], 'scene', [(dev, (dev + 1) % 8) for dev in range(8)])]
    all_gather x1 -> x0, waiting for transfers between devices: 23.1 us -> none  [local(): second_full = lax.all_gather(w_second, 'scene', axis=0, tiled=True)]
    unnamed x10 -> x9, waiting for transfers between devices: 62.3 us -> 61.8 us
    unnamed x73 -> x92, local copies, waits for them, and re-layouts: 15.9 us -> 15.9 us
  transfers between devices with their start and end apart: 8 -> 14, of which waited for: 7 -> 12; matrix products, arithmetic and copies ran while one was open for 16% -> 17% of each run, Pallas kernels for 0% -> 0%
where the time goes in v1:
time: 660 us; the launch traced here: 656 us
  waiting for transfers between devices  403 us (61%)
  local copies, waits for them, and re-layouts  143 us (22%)
  other arithmetic  46.9 us (7%)
  matrix products  22.7 us (3%)
  blocking collectives  22.6 us (3%)
  between operations  17 us (3%)
    psum x1, waiting for transfers between devices, local(): full_first, full_second = lax.psum((grad_first, grad_second), 'region')  165 us
    all_gather x1, waiting for transfers between devices, local(): all_edges = lax.all_gather(edge_rims, 'region', axis=0, tiled=True)  76.7 us
    slice x9, local copies, waits for them, and re-layouts, tap_patches(): padded[:, tap_row:tap_row + stride * out_side:stride, tap_col:tap_col + s...  67.2 us
    all_gather x1, waiting for transfers between devices, local(): all_hidden = lax.all_gather(hidden_rims, 'region', axis=0, tiled=True)  62.6 us
    unnamed x9, waiting for transfers between devices  61.8 us
    gather x22, local copies, waits for them, and re-layouts, fetch(): picked = jnp.take(all_rims, jnp.take(slot_of, position), axis=0)[:, which]  44.9 us
    ppermute x7, waiting for transfers between devices, local(): lax.ppermute(ring[-1], 'scene', [(dev, (dev + 1) % 8) for dev in range(8)])  30.5 us
    unnamed x1, blocking collectives  22.6 us
  transfers between devices with their start and end apart: 14, of which 12 were waited for; matrix products, arithmetic and copies ran while one was open for 17% of the time, Pallas kernels for 0%

profile of v1, /device:TPU:8, one launch (start us, length us, event | category | flops | bytes accessed | tf_op | source)
XLA Modules:
  0.0 656.0 jit_solution(7324868851129761792)
XLA Ops:
  13.1 1.2 and_convert_fusion.2
  14.4 1.3 dynamic-slice
  17.1 22.6 %all-reduce.2 = s32[64]{0:T(128)S(1)} all-reduce(s32[64]{0:T(128)S(1)} %bitcast_dynamic-update-slice_fusion), channel_id=1, replica_groups=mesh['scene'=8,'region'=32] {'region'}, use_global_device_ids=true, to_apply=%add.2 | all-reduce | flops 64 | bytes 512
  46.8 5.2 collective-permute-done.1
  52.6 5.2 collective-permute-done.2
  57.8 5.7 collective-permute-done.3
  64.2 5.2 collective-permute-done.4
  70.5 4.6 collective-permute-done.5
  76.3 4.6 collective-permute-done.6
  81.5 7.2 %all-gather.11.cloned.1.call-done = bf16[64,2,16,256]{3,2,1,0:T(8,128)(2,1)} async-done(((bf16[2,2,16,256]{3,2,1,0:T(8,128)(2,1)}), bf16[64,2,16,256]{3,2,1,0:T(8,128)(2,1)}) %all-gather.11.cloned.1.call-update) | async-done | bytes 1048592 | tf_op jit(solution)/shard_map/all_gather | solution.py:117
  88.7 1.8 gather_fusion.21
  90.6 1.8 gather_fusion.19
  92.6 1.8 gather_fusion.20
  94.4 76.7 %all-gather.5.cloned.1.call-done = bf16[64,4,32,256]{3,2,1,0:T(8,128)(2,1)} async-done(((bf16[2,4,32,256]{3,2,1,0:T(8,128)(2,1)}), bf16[64,4,32,256]{3,2,1,0:T(8,128)(2,1)}) %all-gather.5.cloned.1.call-update) | async-done | bytes 4194320 | tf_op jit(solution)/shard_map/all_gather | solution.py:71
  171.1 2.7 gather_fusion.15
  176.1 1.8 fusion.1
  177.9 3.6 gather_fusion.13
  181.5 1.5 fusion.21
  183.0 3.6 gather_fusion.9
  187.5 1.4 copy_multiply_fusion.2
  188.9 3.6 gather_fusion.1
  193.3 1.3 slice_multiply_fusion.5
  194.5 3.5 gather_fusion.5
  198.9 1.2 slice_multiply_fusion.4
  200.1 3.5 gather_fusion.11
  204.5 1.3 slice_multiply_fusion.3
  205.8 3.5 gather_fusion.7
  210.1 1.4 copy_multiply_fusion.3
  211.5 3.5 gather_fusion.3
  217.3 2.8 pad_maximum_fusion.2
  221.7 3.6 copy.128
  225.3 3.7 copy.138
  229.0 1.7 slice_dynamic-update-slice_fusion.4
  230.7 1.6 slice_dynamic-update-slice_fusion.3
  232.3 1.7 fusion.9
  235.1 1.7 fusion.8
  238.0 1.6 slice_dynamic-update-slice_fusion.1
  239.6 1.6 slice_dynamic-update-slice_fusion
  241.2 8.1 %multiply_convert_fusion = (bf16[2,32,32,256]{3,2,1,0:T(8,128)(2,1)S(1)}, f32[2,32,32,256]{3,2,1,0:T(8,128)}) fusion(bf16[2,32,32,2304]{3,2,1,0:T(8,128)(2,1)} %slice_dynamic-update-slice_fusion, bf16[2304,256]{1,0:T(8,128)(2,1)} %all-gather.7.cloned.1.call-done), kind=kOutput, calls=%fused_computation.36 | convolution fusion | flops 2418540544 | bytes 13762560 | tf_op jit(solution)/shard_map/dot_general | solution.py:85
  249.4 9.9 %slice.204 = bf16[2,16,16,256]{3,2,1,0:T(8,128)(2,1)} slice(bf16[2,32,32,256]{3,2,1,0:T(8,128)(2,1)S(1)} %get-tuple-element.70), slice={[0:2:1], [0:32:2], [0:32:2], [0:256:1]} | slice | bytes 524288 | tf_op jit(solution)/shard_map/slice | solution.py:20
  259.3 9.8 %slice.205 = bf16[2,16,16,256]{3,2,1,0:T(8,128)(2,1)} slice(bf16[2,32,32,256]{3,2,1,0:T(8,128)(2,1)S(1)} %get-tuple-element.70), slice={[0:2:1], [0:32:2], [1:32:2], [0:256:1]} | slice | bytes 524288 | tf_op jit(solution)/shard_map/slice | solution.py:20
  269.1 9.8 %slice.207 = bf16[2,16,16,256]{3,2,1,0:T(8,128)(2,1)} slice(bf16[2,32,32,256]{3,2,1,0:T(8,128)(2,1)S(1)} %get-tuple-element.70), slice={[0:2:1], [1:32:2], [0:32:2], [0:256:1]} | slice | bytes 524288 | tf_op jit(solution)/shard_map/slice | solution.py:20
  278.9 9.8 %slice.208 = bf16[2,16,16,256]{3,2,1,0:T(8,128)(2,1)} slice(bf16[2,32,32,256]{3,2,1,0:T(8,128)(2,1)S(1)} %get-tuple-element.70), slice={[0:2:1], [1:32:2], [1:32:2], [0:256:1]} | slice | bytes 524288 | tf_op jit(solution)/shard_map/slice | solution.py:20
  288.8 2.4 slice_bitcast_fusion.3
  291.9 2.2 fusion.4
  296.8 7.9 %convolution_bitcast_fusion.1 = f32[2304,256]{1,0:T(8,128)} fusion(bf16[2,32,32,2304]{3,2,1,0:T(8,128)(2,1)} %slice_dynamic-update-slice_fusion, f32[2,32,32,256]{3,0,2,1:T(2,128)S(1)} %slice.308, f32[2,32,32,256]{3,2,1,0:T(8,128)S(1)} %copy-done.27), kind=kOutput, calls=%fused_computation.24 | convolution fusion | flops 2420637696 | bytes 15990784 | tf_op jit(solution)/shard_map/dot_general | solution.py:144
  304.8 62.6 %all-gather.9.cloned.1.call-done = bf16[64,2,32,256]{3,2,1,0:T(8,128)(2,1)} async-done(((bf16[2,2,32,256]{3,2,1,0:T(8,128)(2,1)}), bf16[64,2,32,256]{3,2,1,0:T(8,128)(2,1)}) %all-gather.9.cloned.1.call-update) | async-done | bytes 2097168 | tf_op jit(solution)/shard_map/all_gather | solution.py:101
  367.3 2.3 gather_fusion.18
  369.8 1.8 pad_maximum_fusion.3
  371.6 2.3 gather_fusion.16
  374.0 2.3 gather_fusion.17
  380.0 12.5 %slice.203 = bf16[2,16,16,256]{3,2,1,0:T(8,128)(2,1)S(1)} slice(bf16[2,32,33,256]{3,2,1,0:T(8,128)(2,1)} %pad_maximum_fusion.3), slice={[0:2:1], [0:32:2], [0:32:2], [0:256:1]} | slice | bytes 524288 | tf_op jit(solution)/shard_map/slice | solution.py:20
  392.5 12.5 %slice.206 = bf16[2,16,16,256]{3,2,1,0:T(8,128)(2,1)S(1)} slice(bf16[2,32,33,256]{3,2,1,0:T(8,128)(2,1)} %pad_maximum_fusion.3), slice={[0:2:1], [1:32:2], [0:32:2], [0:256:1]} | slice | bytes 524288 | tf_op jit(solution)/shard_map/slice | solution.py:20
  405.3 1.4 copy-done.14
  406.7 2.3 convolution_bitcast_fusion
  409.1 164.6 %all-reduce.6.cloned.1.call-done = (f32[2304,256]{1,0:T(8,128)}, f32[2304,256]{1,0:T(8,128)}) async-done(((f32[2304,256]{1,0:T(8,128)}, f32[2304,256]{1,0:T(8,128)}), (f32[2304,256]{1,0:T(8,128)}, f32[2304,256]{1,0:T(8,128)})) %all-reduce.6.cloned.1.call-update) | async-done | bytes 4718608 | tf_op jit(solution)/shard_map/psum | solution.py:151
  573.8 3.0 multiply_reduce_fusion
  576.8 1.2 multiply_reduce_fusion.1
  579.4 1.5 dynamic-slice_multiply_fusion
  580.9 1.6 copy.141
  583.3 1.6 copy.139
  584.9 3.1 convolution_convert_fusion
  588.1 26.2 %reduce-scatter.9.cloned.1.call-done = f32[32,72]{1,0:T(8,128)} async-done(((f32[256,72]{1,0:T(8,128)}), f32[32,72]{1,0:T(8,128)}) %reduce-scatter.9.cloned.1.call-update) | async-done | bytes 9232
  614.3 34.8 %reduce-scatter.7.cloned.1.call-done = f32[32,72]{1,0:T(8,128)} async-done(((f32[256,72]{1,0:T(8,128)}), f32[32,72]{1,0:T(8,128)}) %reduce-scatter.7.cloned.1.call-update) | async-done | bytes 9232
  (185 shorter events, 39.0 us)
Async XLA Ops:
  7.2 81.6 %all-gather.11.cloned.1.call-start = ((), (), s32[]{:S(2)}) async-start(), calls=%async_computation.5 | async-start | bytes 1081344 | tf_op jit(solution)/shard_map/all_gather | solution.py:117
  8.9 165.7 %copy-start.5 = (bf16[2,16,16,256]{3,2,1,0:T(8,128)(2,1)}, bf16[2,16,16,256]{3,2,1,0:T(8,128)(2,1)S(1)}, u32[]{:S(2)}) copy-start(bf16[2,16,16,256]{3,2,1,0:T(8,128)(2,1)S(1)} %bitcast_multiply_fusion) | copy-start | bytes 786436
  9.6 161.4 %all-gather.5.cloned.1.call-start = ((), (), s32[]{:S(2)}) async-start(), calls=%async_computation.2 | async-start | bytes 4325376 | tf_op jit(solution)/shard_map/all_gather | solution.py:71
  12.3 228.8 %all-gather.7.cloned.1.call-start = ((), (), s32[]{:S(2)}) async-start(), calls=%async_computation.3 | async-start | bytes 1327104 | tf_op jit(solution)/shard_map/all_gather | solution.py:87
  12.4 33.8 %collective-permute-start = (bf16[288,256]{1,0:T(8,128)(2,1)}, bf16[288,256]{1,0:T(8,128)(2,1)S(1)}, u32[]{:S(2)}, u32[]{:S(2)}) collective-permute-start(bf16[288,256]{1,0:T(8,128)(2,1)} %param.19), channel_id=1, source_target_pairs={{0,32},{32,64},{64,96},{96,128},{128,160},{160,192},{192,224},{224... | collective-permute-start | bytes 442376 | tf_op jit(solution)/shard_map/ppermute | solution.py:92
  13.1 354.2 %all-gather.9.cloned.1.call-start = ((), (), s32[]{:S(2)}) async-start(), calls=%async_computation.4 | async-start | bytes 2162688 | tf_op jit(solution)/shard_map/all_gather | solution.py:101
  42.3 50.0 %copy-start.23 = (pred[2]{0:T(512)(128)(4,1)}, pred[2]{0:T(512)(128)(4,1)S(1)}, u32[]{:S(2)}) copy-start(pred[2]{0:T(512)(128)(4,1)S(1)} %get-tuple-element.41) | copy-start | bytes 10
  42.3 50.1 %copy-start.22 = (bf16[2]{0:T(256)(128)(2,1)}, bf16[2]{0:T(256)(128)(2,1)S(1)}, u32[]{:S(2)}) copy-start(bf16[2]{0:T(256)(128)(2,1)S(1)} %get-tuple-element.78) | copy-start | bytes 16
  42.3 52.0 %copy-start.24 = (bf16[2]{0:T(256)(128)(2,1)}, bf16[2]{0:T(256)(128)(2,1)S(1)}, u32[]{:S(2)}) copy-start(bf16[2]{0:T(256)(128)(2,1)S(1)} %get-tuple-element.82) | copy-start | bytes 16
  42.4 38.7 %copy-start.13 = (bf16[288,256]{1,0:T(8,128)(2,1)S(1)}, bf16[288,256]{1,0:T(8,128)(2,1)}, u32[]{:S(2)}) copy-start(bf16[288,256]{1,0:T(8,128)(2,1)} %param.19) | copy-start | bytes 442372
  45.6 48.7 %copy-start.25 = (pred[2]{0:T(512)(128)(4,1)}, pred[2]{0:T(512)(128)(4,1)S(1)}, u32[]{:S(2)}) copy-start(pred[2]{0:T(512)(128)(4,1)S(1)} %get-tuple-element.74) | copy-start | bytes 10
  46.2 5.8 collective-permute-start.1
  52.0 5.8 collective-permute-start.2
  57.8 5.8 collective-permute-start.3
  57.8 34.8 %copy-start.15 = (s32[1024]{0:T(1024)}, s32[1024]{0:T(1024)S(1)}, u32[]{:S(2)}) copy-start(s32[1024]{0:T(1024)S(1)} %pad_clamp_fusion.2) | copy-start | bytes 12292
  63.5 5.8 collective-permute-start.4
  63.6 27.0 %copy-start.16 = (s32[1024]{0:T(1024)}, s32[1024]{0:T(1024)S(1)}, u32[]{:S(2)}) copy-start(s32[1024]{0:T(1024)S(1)} %pad_clamp_fusion.6) | copy-start | bytes 12292
  69.3 5.8 collective-permute-start.5
  75.1 5.8 collective-permute-start.6
  81.5 93.1 %copy-start.2 = (bf16[2304,256]{1,0:T(8,128)(2,1)}, bf16[2304,256]{1,0:T(8,128)(2,1)S(1)}, u32[]{:S(2)}) copy-start(bf16[2304,256]{1,0:T(8,128)(2,1)S(1)} %constant_dynamic-slice_fusion) | copy-start | bytes 3538948
  177.9 39.4 %copy-start = (bf16[1,2,32,32,256]{4,3,2,1,0:T(8,128)(2,1)S(1)}, bf16[1,2,32,32,256]{4,3,2,1,0:T(8,128)(2,1)}, u32[]{:S(2)}) copy-start(bf16[1,2,32,32,256]{4,3,2,1,0:T(8,128)(2,1)} %param.14) | copy-start | bytes 3145732
  217.3 4.0 copy-start.1
  229.0 3.3 copy-start.12
  232.3 2.8 copy-start.11
  291.9 281.9 %all-reduce.6.cloned.1.call-start = ((), (), s32[]{:S(2)}) async-start(), calls=%async_computation.8 | async-start | bytes 9437184 | tf_op jit(solution)/shard_map/psum | solution.py:151
  295.2 1.6 copy-start.27
  296.8 72.8 %copy-start.21 = (pred[2]{0:T(512)(128)(4,1)S(1)}, pred[2]{0:T(512)(128)(4,1)}, u32[]{:S(2)}) copy-start(pred[2]{0:T(512)(128)(4,1)} %get-tuple-element.39) | copy-start | bytes 10
  296.8 72.9 %copy-start.19 = (bf16[2]{0:T(256)(128)(2,1)S(1)}, bf16[2]{0:T(256)(128)(2,1)}, u32[]{:S(2)}) copy-start(bf16[2]{0:T(256)(128)(2,1)} %get-tuple-element.81) | copy-start | bytes 16
  304.8 69.1 %copy-start.20 = (pred[2]{0:T(512)(128)(4,1)S(1)}, pred[2]{0:T(512)(128)(4,1)}, u32[]{:S(2)}) copy-start(pred[2]{0:T(512)(128)(4,1)} %get-tuple-element.33) | copy-start | bytes 10
  304.8 69.2 %copy-start.26 = (bf16[2]{0:T(256)(128)(2,1)S(1)}, bf16[2]{0:T(256)(128)(2,1)}, u32[]{:S(2)}) copy-start(bf16[2]{0:T(256)(128)(2,1)} %get-tuple-element.80) | copy-start | bytes 16
  304.8 71.6 %copy-start.17 = (pred[2]{0:T(512)(128)(4,1)S(1)}, pred[2]{0:T(512)(128)(4,1)}, u32[]{:S(2)}) copy-start(pred[2]{0:T(512)(128)(4,1)} %get-tuple-element.35) | copy-start | bytes 10
  304.8 71.6 %copy-start.18 = (bf16[2]{0:T(256)(128)(2,1)S(1)}, bf16[2]{0:T(256)(128)(2,1)}, u32[]{:S(2)}) copy-start(bf16[2]{0:T(256)(128)(2,1)} %get-tuple-element.76) | copy-start | bytes 16
  377.1 28.0 %copy-start.10 = (bf16[2,16,16,256]{3,2,1,0:T(8,128)(2,1)S(1)}, bf16[2,16,16,256]{3,2,1,0:T(8,128)(2,1)}, u32[]{:S(2)}) copy-start(bf16[2,16,16,256]{3,2,1,0:T(8,128)(2,1)} %slice.204) | copy-start | bytes 786436
  378.0 27.2 %copy-start.9 = (bf16[2,16,16,256]{3,2,1,0:T(8,128)(2,1)S(1)}, bf16[2,16,16,256]{3,2,1,0:T(8,128)(2,1)}, u32[]{:S(2)}) copy-start(bf16[2,16,16,256]{3,2,1,0:T(8,128)(2,1)} %slice.205) | copy-start | bytes 786436
  380.0 25.3 %copy-start.8 = (bf16[2,16,16,256]{3,2,1,0:T(8,128)(2,1)S(1)}, bf16[2,16,16,256]{3,2,1,0:T(8,128)(2,1)}, u32[]{:S(2)}) copy-start(bf16[2,16,16,256]{3,2,1,0:T(8,128)(2,1)} %slice.207) | copy-start | bytes 786436
  392.5 12.8 %copy-start.7 = (bf16[2,16,16,256]{3,2,1,0:T(8,128)(2,1)S(1)}, bf16[2,16,16,256]{3,2,1,0:T(8,128)(2,1)}, u32[]{:S(2)}) copy-start(bf16[2,16,16,256]{3,2,1,0:T(8,128)(2,1)} %slice.208) | copy-start | bytes 786436
  405.0 1.7 copy-start.6
  405.3 1.4 copy-start.14
  409.1 205.3 %reduce-scatter.9.cloned.1.call-start = ((), (), s32[]{:S(2)}) async-start(), calls=%async_computation.7 | async-start | bytes 147456
  573.8 3.0 copy-start.4
  573.8 11.2 %copy-start.3 = (bf16[2304,256]{1,0:T(8,128)(2,1)S(1)}, bf16[2304,256]{1,0:T(8,128)(2,1)}, u32[]{:S(2)}) copy-start(bf16[2304,256]{1,0:T(8,128)(2,1)} %copy-done.2) | copy-start | bytes 3538948
  582.6 66.6 %reduce-scatter.7.cloned.1.call-start = ((), (), s32[]{:S(2)}) async-start(), calls=%async_computation.6 | async-start | bytes 147456
Sparse Core Ops, SparseCore 0:
  10.6 78.0 all-gather.10
  91.9 79.1 all-gather.4
  172.9 24.6 all-gather.6
  292.0 75.2 all-gather.8
  409.2 164.5 all-reduce.5
  582.7 31.5 reduce-scatter.8
  617.4 31.6 reduce-scatter.6
